TPU v7x, 32 devices: a whole 2x2x4 slice. The times are simulated.
32 devices in a mesh: exp: 4 (over y, x), dp: 8 (over z, core).
Axes of the slice: x: 2, y: 2, z: 4, core: 2. Of those that a mesh axis runs over, the one named last changes fastest.
Arguments:
- expert_inputs: bfloat16 [4, 2048, 2048], P('exp', 'dp'), may hold values from -6 to 6
- hidden_grads: bfloat16 [4, 2048, 7168], P('exp', 'dp'), may hold values from -0.125 to 0.125
- expert_weight: float32 [4, 2048, 7168], P('exp', 'dp'), may hold values from -0.125 to 0.125
- expert_moment: bfloat16 [4, 2048, 7168], P('exp', 'dp'), may hold values from -4 to 4
- expert_second: bfloat16 [4, 2048, 7168], P('exp', 'dp'), may hold values from 0.0009994507 to 1
- key_partial: float32 [4, 2048, 512], P('exp', 'dp'), may hold values from -5 to 5
- key_weight: float32 [2048, 512], P('dp'), may hold values from -0.125 to 0.125
- key_moment: float32 [4, 512, 512], P('exp', 'dp'), may hold values from -4 to 4
- key_second: float32 [4, 512, 512], P('exp', 'dp'), may hold values from 0.001 to 1
- slice_owner: int32 [4], replicated, may hold values from 0 to 3, each once
Outputs:
- expert_weight_next: float32 [4, 2048, 7168], P('exp', 'dp')
- expert_moment_next: bfloat16 [4, 2048, 7168], P('exp', 'dp')
- expert_second_next: bfloat16 [4, 2048, 7168], P('exp', 'dp')
- key_weight_next: float32 [2048, 512], P('dp')
- key_moment_next: float32 [4, 512, 512], P('exp', 'dp')
- key_second_next: float32 [4, 512, 512], P('exp', 'dp')
Inputs may be any that keep to these rules, and one draw needn't show every extreme that they name: `slice_owner`: each exp group holds exactly one slice.
All inputs are finite; a program needn't handle non-finite values.
Results may differ from a plain program's by a relative error of at most 0.012.
Values may be sent and summed in bfloat16 or wider, within the bound.
A program may use at most 192 MiB of HBM per device.

v0:
```python
import jax
import jax.numpy as jnp
from jax import lax
from jax.sharding import PartitionSpec as P

STEP = 10


first_decay = 0.9
second_decay = 0.999
learn_rate = 0.01
weight_decay = 0.1
epsilon = 1e-08


def adam_update(param, moment, second, gradient):
    moment_new = first_decay * moment.astype(jnp.float32) + (1.0 - first_decay) * gradient
    second_new = (
        second_decay * second.astype(jnp.float32) + (1.0 - second_decay) * gradient * gradient
    )
    moment_hat = moment_new / (1.0 - first_decay**STEP)
    second_hat = second_new / (1.0 - second_decay**STEP)
    param_new = param - learn_rate * (
        moment_hat / (jnp.sqrt(second_hat) + epsilon) + weight_decay * param
    )
    return (param_new, moment_new, second_new)


def shards(
    expert_inputs,
    hidden_grads,
    expert_weight,
    expert_moment,
    expert_second,
    key_partial,
    key_weight,
    key_moment,
    key_second,
    slice_owner,
):
    inputs = expert_inputs[0]
    upstream = hidden_grads[0]
    gradient = lax.psum_scatter(
        lax.dot_general(
            inputs, upstream, (((0,), (0,)), ((), ())), preferred_element_type=jnp.float32
        ).astype(jnp.bfloat16),
        "dp",
        scatter_dimension=0,
        tiled=True,
    ).astype(jnp.float32)
    weight_next, moment_f, second_f = adam_update(
        expert_weight[0], expert_moment[0], expert_second[0], gradient
    )
    moment_next = moment_f.astype(jnp.bfloat16)
    second_next = second_f.astype(jnp.bfloat16)
    groups = lax.axis_size("exp")
    holder = lax.axis_index("exp")
    shard_rows = key_weight.shape[0]
    slice_rows = shard_rows // groups
    columns_key = key_weight.shape[1]
    picker = (slice_owner[None, :] == jnp.arange(groups, dtype=jnp.int32)[:, None]).astype(
        jnp.float32
    )
    flat_partial = key_partial[0].reshape(groups, slice_rows * columns_key)
    arranged = jnp.dot(
        picker, flat_partial, precision=lax.Precision.HIGHEST, preferred_element_type=jnp.float32
    )
    key_gradient = (
        lax.psum_scatter(arranged.astype(jnp.bfloat16), "exp", scatter_dimension=0, tiled=True)
        .astype(jnp.float32)
        .reshape(slice_rows, columns_key)
    )
    held_slice = jnp.sum(jnp.where(slice_owner == holder, jnp.arange(groups, dtype=jnp.int32), 0))
    old_slice = lax.dynamic_slice_in_dim(key_weight, held_slice * slice_rows, slice_rows, 0)
    slice_new, key_moment_new, key_second_new = adam_update(
        old_slice, key_moment[0], key_second[0], key_gradient
    )
    gathered = lax.all_gather(slice_new, "exp", axis=0, tiled=True).reshape(
        groups, slice_rows * columns_key
    )
    ordered = jnp.dot(
        picker.T, gathered, precision=lax.Precision.HIGHEST, preferred_element_type=jnp.float32
    )
    key_next = ordered.reshape(shard_rows, columns_key)
    return (
        weight_next[None],
        moment_next[None],
        second_next[None],
        key_next,
        key_moment_new[None],
        key_second_new[None],
    )


def solution(mesh):
    in_specs = (
        P("exp", "dp", None),
        P("exp", "dp", None),
        P("exp", "dp", None),
        P("exp", "dp", None),
        P("exp", "dp", None),
        P("exp", "dp", None),
        P("dp", None),
        P("exp", "dp", None),
        P("exp", "dp", None),
        P(),
    )
    out_specs = (
        P("exp", "dp", None),
        P("exp", "dp", None),
        P("exp", "dp", None),
        P("dp", None),
        P("exp", "dp", None),
        P("exp", "dp", None),
    )
    return jax.shard_map(shards, mesh=mesh, in_specs=in_specs, out_specs=out_specs, check_vma=False)
```

profile of v0, /device:TPU:0, one launch (start us, length us, event | category | flops | bytes accessed | tf_op | source)
XLA Modules:
  0.0 337.6 jit_solution(11111455229716052655)
XLA Ops:
  8.0 0.0 copy-start
  8.0 0.0 all-reduce.3.cloned.1.call-start
  8.1 1.5 reshape_squeeze.3
  9.5 2.0 convolution_convert_fusion
  11.5 0.0 all-reduce.3.cloned.1.call-update
  11.5 0.0 reduce-scatter.2.cloned.1.call-start
  11.6 0.0 copy-done
  11.6 14.5 %convolution_convert_fusion.1 = bf16[2048,7168]{1,0:T(8,128)(2,1)} fusion(bf16[1,256,7168]{2,1,0:T(8,128)(2,1)} %param.11, bf16[1,256,2048]{2,1,0:T(8,128)(2,1)S(1)} %copy-done), kind=kOutput, calls=%fused_computation.1 | convolution fusion | flops 7530872832 | bytes 34078720 | tf_op jit(solution)/shard_map/dot_general | solution.py:44
  26.1 0.0 copy-start.4
  26.1 0.0 copy-start.5
  26.1 0.0 copy-start.2
  26.1 0.0 copy-start.3
  26.1 0.0 reduce-scatter.2.cloned.1.call-update
  26.2 0.6 copy-done.4
  26.8 0.6 fusion.22
  28.1 0.0 copy-done.5
  28.1 0.6 dynamic-slice
  28.7 29.5 %all-reduce.3.cloned.1.call-done = bf16[4,32768]{1,0:T(4,128)(2,1)} async-done(((bf16[4,32768]{1,0:T(4,128)(2,1)}), bf16[4,32768]{1,0:T(4,128)(2,1)}) %all-reduce.3.cloned.1.call-update) | async-done | bytes 262160
  58.1 0.5 broadcast.49
  58.6 2.6 fusion.23
  61.3 0.0 copy-done.2
  61.3 0.0 copy-done.3
  61.3 1.0 multiply_subtract_fusion
  62.4 10.0 %all_gather.3 = f32[256,512]{1,0:T(8,128)S(1)} all-gather(f32[64,512]{1,0:T(8,128)S(1)} %multiply_subtract_fusion), channel_id=1, replica_groups=mesh['exp'=4,'dp'=8] {'exp'}, dimensions={0}, use_global_device_ids=true | all-gather | bytes 655360 | tf_op jit(solution)/shard_map/all_gather | solution.py:78
  72.4 0.4 reshape.64
  72.7 0.7 fusion.19
  73.4 1.2 reshape.65
  74.6 0.7 fusion.17
  75.4 240.1 %reduce-scatter.2.cloned.1.call-done = bf16[256,7168]{1,0:T(8,128)(2,1)} async-done(((bf16[2048,7168]{1,0:T(8,128)(2,1)}), bf16[256,7168]{1,0:T(8,128)(2,1)}) %reduce-scatter.2.cloned.1.call-update) | async-done | bytes 3670032 | tf_op jit(solution)/shard_map/reduce_scatter | solution.py:43
  315.4 0.0 copy-start.1
  315.4 14.8 %fusion.7 = (bf16[1,256,7168]{2,1,0:T(8,128)(2,1)}, f32[1,256,7168]{2,1,0:T(8,128)}, bf16[1,256,7168]{2,1,0:T(8,128)(2,1)}) fusion(bf16[256,7168]{1,0:T(8,128)(2,1)} %reduce-scatter.2.cloned.1.call-done, bf16[1,256,7168]{2,1,0:T(8,128)(2,1)} %param.14, bf16[1,256,7168]{2,1,0:T(8,128)(2,1)} %param.13, f32[1,256,7168]{2,1,0:T(8,128)} %param.12), kind=kLoop, calls=%fused_computation.13 | loop fusion | flops 36700160 | bytes 33030144 | tf_op jit(solution)/shard_map/broadcast_in_dim | solution.py:88
  330.2 0.0 copy-done.1
  (2 shorter events, 0.0 us)
Async XLA Ops:
  8.0 3.6 %copy-start = (bf16[1,256,2048]{2,1,0:T(8,128)(2,1)S(1)}, bf16[1,256,2048]{2,1,0:T(8,128)(2,1)}, u32[]{:S(2)}) copy-start(bf16[1,256,2048]{2,1,0:T(8,128)(2,1)} %param.10) | copy-start | bytes 3145732
  8.0 50.1 %all-reduce.3.cloned.1.call-start = ((), (), s32[]{:S(2)}) async-start(), calls=%async_computation.2 | async-start | bytes 524288
  11.5 303.9 %reduce-scatter.2.cloned.1.call-start = ((), (), s32[]{:S(2)}) async-start(), calls=%async_computation.1 | async-start | bytes 33030144 | tf_op jit(solution)/shard_map/reduce_scatter | solution.py:43
  26.1 0.7 copy-start.4
  26.1 1.9 copy-start.5
  26.1 35.2 %copy-start.2 = (f32[1,64,512]{2,1,0:T(8,128)S(1)}, f32[1,64,512]{2,1,0:T(8,128)}, u32[]{:S(2)}) copy-start(f32[1,64,512]{2,1,0:T(8,128)} %param.18) | copy-start | bytes 393220
  26.1 35.2 %copy-start.3 = (f32[1,64,512]{2,1,0:T(8,128)S(1)}, f32[1,64,512]{2,1,0:T(8,128)}, u32[]{:S(2)}) copy-start(f32[1,64,512]{2,1,0:T(8,128)} %param.17) | copy-start | bytes 393220
  315.4 14.8 %copy-start.1 = (bf16[1,256,2048]{2,1,0:T(8,128)(2,1)S(1)}, bf16[1,256,2048]{2,1,0:T(8,128)(2,1)}, u32[]{:S(2)}) copy-start(bf16[1,256,2048]{2,1,0:T(8,128)(2,1)} %param.10) | copy-start | bytes 3145732
Sparse Core Ops, SparseCore 0:
  12.3 45.7 all-reduce.2
Sparse Core Ops, SparseCore 1:
  26.2 289.1 reduce-scatter.1
where the time goes:
time: 338 us
  waiting for transfers between devices  270 us (80%)
  other arithmetic  19.8 us (6%)
  matrix products  17.2 us (5%)
  between operations  16.2 us (5%)
  blocking collectives  9.99 us (3%)
  local copies, waits for them, and re-layouts  4.75 us (1%)
    reduce_scatter x1, waiting for transfers between devices, shards(): lax.psum_scatter(lax.dot_general(inputs, upstream, (((0,), (0,)), ((), ()...  240 us
    unnamed x3, waiting for transfers between devices  29.5 us
    broadcast_in_dim x1, other arithmetic, shards(): second_next[None]  14.8 us
    dot_general x1, matrix products, shards(): lax.dot_general(inputs, upstream, (((0,), (0,)), ((), ())), preferred_ele...  14.5 us
    all_gather x1, blocking collectives, shards(): lax.all_gather(slice_new, 'exp', axis=0, tiled=True)  9.99 us
  transfers between devices with their start and end apart: 2, of which 2 were waited for; matrix products, arithmetic and copies ran while one was open for 7% of the time, Pallas kernels for 0%

commit v1 on v0

--- a/solution.py
+++ b/solution.py
@@ -1,6 +1,10 @@
+import functools
+
 import jax
 import jax.numpy as jnp
 from jax import lax
+from jax.experimental import pallas as pl
+from jax.experimental.pallas import tpu as pltpu
 from jax.sharding import PartitionSpec as P
 
 STEP = 10
@@ -92,6 +96,415 @@
     )
 
 
+MESH = pl.DeviceIdType.MESH
+CHAIN = 4
+
+
+def kernel(
+    chunk,
+    in_ref,
+    hid_ref,
+    karr_ref,
+    kold_ref,
+    kmom_ref,
+    ksec_ref,
+    g_ref,
+    kall_ref,
+    kmom_out,
+    ksec_out,
+    lhs,
+    rhs,
+    prod,
+    got,
+    fwd,
+    own,
+    kgot,
+    local_sem,
+    swap_send,
+    swap_recv,
+    fact_send,
+    fact_recv,
+    far_send,
+    far_recv,
+    near_send,
+    near_recv,
+    out_sem,
+    out_send,
+    out_recv,
+    lhs_send,
+    lhs_recv,
+    edge_send,
+    edge_recv,
+    pass_send,
+    pass_recv,
+    key_send,
+    key_recv,
+    all_send,
+    all_recv,
+):
+    exp = lax.axis_index("exp")
+    groups = lax.axis_size("exp")
+    place = lax.axis_index("dp")
+    chip = place // 2
+    core = place % 2
+    other = 1 - core
+    partner = (exp, chip * 2 + other)
+    tokens, width = in_ref.shape
+    rows = width // (2 * CHAIN)
+    block = 2 * rows
+    half = hid_ref.shape[1] // 2
+    count = half // chunk
+    middle = (chip == 1) | (chip == 2)
+    outer = (chip // 2) * (CHAIN - 1)
+    far = CHAIN - 1 - outer
+    inner = 1 + (1 - chip // 2)
+    near = 1 + chip // 2
+    outer_dev = (exp, outer * 2 + core)
+    inner_dev = (exp, inner * 2 + core)
+    near_dev = (exp, near * 2 + core)
+
+    def remote(src, dst, send, recv, dev):
+        return pltpu.make_async_remote_copy(
+            src_ref=src, dst_ref=dst, send_sem=send, recv_sem=recv, device_id=dev,
+            device_id_type=MESH,
+        )
+
+    def rows_of(which):
+        return pl.ds(pl.multiple_of(which * block, block), block)
+
+    def columns(side, c):
+        return pl.ds(pl.multiple_of(side * half + c * chunk, chunk), chunk)
+
+    def matmul(which, c, depth):
+        return jnp.dot(
+            lhs[rows_of(which), 0:depth], rhs[c, 0:depth, :], preferred_element_type=jnp.float32
+        )
+
+    def local_copy(c):
+        return pltpu.make_async_copy(
+            hid_ref.at[:, columns(core, c)], rhs.at[c, pl.ds(0, tokens)], local_sem.at[c]
+        )
+
+    def swap_copy(c):
+        return remote(
+            hid_ref.at[:, columns(other, c)], rhs.at[c, pl.ds(tokens, tokens)],
+            swap_send.at[c], swap_recv.at[c], partner,
+        )
+
+    def factor_copy(c):
+        return remote(
+            rhs.at[c, pl.ds(0, 2 * tokens)], rhs.at[c, pl.ds(2 * tokens, 2 * tokens)],
+            fact_send.at[c], fact_recv.at[c], near_dev,
+        )
+
+    def far_copy(c):
+        return remote(
+            prod.at[c, pl.ds(0, block)], got.at[c, pl.ds(0, block)],
+            far_send.at[c], far_recv.at[c], inner_dev,
+        )
+
+    def near_copy(c):
+        return remote(
+            prod.at[c, pl.ds(block, block)], got.at[c, pl.ds(block, block)],
+            near_send.at[c], near_recv.at[c], inner_dev,
+        )
+
+    def edge_result(c):
+        return remote(
+            fwd.at[c], got.at[c, pl.ds(block, block)], far_recv_send(c), near_recv.at[c], outer_dev
+        )
+
+    def far_recv_send(c):
+        return fact_send.at[c]
+
+    def out_copy(c):
+        return pltpu.make_async_copy(
+            own.at[c, pl.ds(pl.multiple_of(core * rows, rows), rows)],
+            g_ref.at[:, columns(core, c)], out_sem.at[c],
+        )
+
+    def out_swap(c):
+        return remote(
+            own.at[c, pl.ds(pl.multiple_of(other * rows, rows), rows)],
+            g_ref.at[:, columns(core, c)], out_send.at[c], out_recv.at[c], partner,
+        )
+
+    lhs_swap = remote(
+        lhs.at[:, pl.ds(0, tokens)], lhs.at[:, pl.ds(tokens, tokens)],
+        lhs_send, lhs_recv, partner,
+    )
+
+    def part_of(k):
+        return (far, inner, near)[k]
+
+    def edge_copy(k):
+        at = rows_of(part_of(k))
+        return remote(
+            lhs.at[at, pl.ds(0, tokens)], lhs.at[at, pl.ds(2 * tokens, tokens)],
+            edge_send.at[k], edge_recv.at[k], near_dev,
+        )
+
+    def pass_copy(k):
+        at = rows_of(part_of(k))
+        return remote(
+            lhs.at[at, pl.ds(2 * tokens, tokens)], lhs.at[at, pl.ds(3 * tokens, tokens)],
+            pass_send.at[k], pass_recv.at[k], partner,
+        )
+
+    def key_copy(d):
+        peer = lax.rem(exp + d, groups)
+        return remote(
+            karr_ref.at[peer], kgot.at[d - 1], key_send.at[d - 1], key_recv.at[d - 1],
+            (peer, place),
+        )
+
+    def all_copy(d):
+        peer = lax.rem(exp + d, groups)
+        return remote(
+            kall_ref.at[exp], kall_ref.at[exp], all_send.at[d - 1], all_recv.at[d - 1],
+            (peer, place),
+        )
+
+    def all_arrival(d):
+        source = lax.rem(exp + groups - d, groups)
+        return remote(
+            kall_ref.at[source], kall_ref.at[source], all_send.at[d - 1], all_recv.at[d - 1],
+            (source, place),
+        )
+
+    barrier = pltpu.get_barrier_semaphore()
+
+    def greet(dev):
+        pl.semaphore_signal(barrier, inc=1, device_id=dev, device_id_type=MESH)
+
+    greet(partner)
+    for d in range(1, groups):
+        greet((lax.rem(exp + d, groups), place))
+
+    @pl.when(middle)
+    def _():
+        greet(outer_dev)
+        greet(inner_dev)
+        pl.semaphore_wait(barrier, groups + 2)
+
+    @pl.when(jnp.logical_not(middle))
+    def _():
+        greet(near_dev)
+        pl.semaphore_wait(barrier, groups + 1)
+
+    @pl.loop(0, count)
+    def _(c):
+        local_copy(c).start()
+        swap_copy(c).start()
+
+    @pl.loop(0, 2 * CHAIN)
+    def _(q):
+        at = pl.ds(pl.multiple_of(q * rows, rows), rows)
+        lhs[at, 0:tokens] = in_ref[:, at].T
+
+    @pl.when(jnp.logical_not(middle))
+    def _():
+        for k in range(3):
+            edge_copy(k).start()
+
+    lhs_swap.start()
+    for d in range(1, groups):
+        key_copy(d).start()
+
+    def key_step():
+        for d in range(1, groups):
+            key_copy(d).wait_recv()
+        total = karr_ref[exp].astype(jnp.float32)
+        for d in range(1, groups):
+            total += kgot[d - 1].astype(jnp.float32)
+        new, moment, second = adam_update(kold_ref[...], kmom_ref[...], ksec_ref[...], total)
+        kmom_out[...] = moment
+        ksec_out[...] = second
+        kall_ref[exp] = new
+        for d in range(1, groups):
+            all_copy(d).start()
+
+    def finish(c, depth):
+        own[c] = (matmul(chip, c, depth) + got[c, block:, :].astype(jnp.float32)).astype(own.dtype)
+        out_copy(c).start()
+        out_swap(c).start()
+
+    @pl.when(jnp.logical_not(middle))
+    def _():
+        @pl.loop(0, count)
+        def _(c):
+            local_copy(c).wait()
+            swap_copy(c).wait_recv()
+            factor_copy(c).start()
+
+        lhs_swap.wait_recv()
+        key_step()
+
+        @pl.loop(0, count)
+        def _(c):
+            near_copy(c).wait_recv()
+            finish(c, 2 * tokens)
+
+        @pl.loop(0, count)
+        def _(c):
+            factor_copy(c).wait_send()
+
+        for k in range(3):
+            edge_copy(k).wait_send()
+
+    @pl.when(middle)
+    def _():
+        for k in range(3):
+            edge_copy(k).wait_recv()
+            pass_copy(k).start()
+        lhs_swap.wait_recv()
+        for k in range(3):
+            pass_copy(k).wait_recv()
+
+        @pl.loop(0, count + 1)
+        def _(c):
+            @pl.when(c < count)
+            def _():
+                local_copy(c).wait()
+                swap_copy(c).wait_recv()
+                factor_copy(c).wait_recv()
+                prod[c, 0:block, :] = matmul(far, c, 4 * tokens).astype(prod.dtype)
+                far_copy(c).start()
+                prod[c, block:, :] = matmul(inner, c, 4 * tokens).astype(prod.dtype)
+                near_copy(c).start()
+
+            @pl.when(c == 1)
+            def _():
+                key_step()
+
+            @pl.when(c > 0)
+            def _():
+                p = c - 1
+                far_copy(p).wait_recv()
+                fwd[p] = (
+                    matmul(outer, p, 2 * tokens) + got[p, 0:block, :].astype(jnp.float32)
+                ).astype(fwd.dtype)
+                edge_result(p).start()
+                near_copy(p).wait_recv()
+                finish(p, 4 * tokens)
+
+        @pl.loop(0, count)
+        def _(c):
+            far_copy(c).wait_send()
+            near_copy(c).wait_send()
+            edge_result(c).wait_send()
+
+        for k in range(3):
+            pass_copy(k).wait_send()
+
+    lhs_swap.wait_send()
+    for d in range(1, groups):
+        key_copy(d).wait_send()
+        all_copy(d).wait_send()
+        all_arrival(d).wait_recv()
+
+    @pl.loop(0, count)
+    def _(c):
+        swap_copy(c).wait_send()
+        out_copy(c).wait()
+        out_swap(c).wait_send()
+        remote(
+            own.at[c, pl.ds(0, rows)], g_ref.at[:, columns(other, c)],
+            out_send.at[c], out_recv.at[c], partner,
+        ).wait_recv()
+
+
+def chained(inputs, upstream, arranged, key_old, key_moment, key_second):
+    tokens, width = inputs.shape
+    columns = upstream.shape[1]
+    half = columns // 2
+    chunk = 256 if half % 256 == 0 else 128
+    count = half // chunk
+    block = width // CHAIN
+    groups = arranged.shape[0]
+    vmem = pl.BlockSpec(memory_space=pltpu.VMEM)
+    hbm = pl.BlockSpec(memory_space=pl.ANY)
+    key_shape = jax.ShapeDtypeStruct(key_old.shape, jnp.float32)
+    dma = pltpu.SemaphoreType.DMA
+    return pl.pallas_call(
+        functools.partial(kernel, chunk),
+        out_shape=(
+            jax.ShapeDtypeStruct((width // (2 * CHAIN), columns), jnp.bfloat16),
+            jax.ShapeDtypeStruct((groups,) + key_old.shape, jnp.float32),
+            key_shape,
+            key_shape,
+        ),
+        in_specs=[vmem, hbm, vmem, vmem, vmem, vmem],
+        out_specs=(hbm, vmem, vmem, vmem),
+        scratch_shapes=[
+            pltpu.VMEM((width, 4 * tokens), jnp.bfloat16),
+            pltpu.VMEM((count, 4 * tokens, chunk), jnp.bfloat16),
+            pltpu.VMEM((count, 2 * block, chunk), jnp.bfloat16),
+            pltpu.VMEM((count, 2 * block, chunk), jnp.bfloat16),
+            pltpu.VMEM((count, block, chunk), jnp.bfloat16),
+            pltpu.VMEM((count, block, chunk), jnp.bfloat16),
+            pltpu.VMEM((groups - 1,) + key_old.shape, jnp.bfloat16),
+        ]
+        + [dma((count,))] * 12
+        + [dma, dma]
+        + [dma((3,))] * 4
+        + [dma((groups - 1,))] * 4,
+        compiler_params=pltpu.CompilerParams(
+            collective_id=0, has_side_effects=True, vmem_limit_bytes=60 * 1024 * 1024
+        ),
+        cost_estimate=pl.CostEstimate(
+            flops=14 * block * block * half, bytes_accessed=4 * width * columns, transcendentals=0
+        ),
+    )(inputs, upstream, arranged, key_old, key_moment, key_second)
+
+
+def line_shards(
+    expert_inputs,
+    hidden_grads,
+    expert_weight,
+    expert_moment,
+    expert_second,
+    key_partial,
+    key_weight,
+    key_moment,
+    key_second,
+    slice_owner,
+):
+    groups = lax.axis_size("exp")
+    holder = lax.axis_index("exp")
+    slice_rows = key_weight.shape[0] // groups
+    columns_key = key_weight.shape[1]
+    index = jnp.arange(groups, dtype=jnp.int32)
+
+    def pick(mask, blocks):
+        return jnp.sum(jnp.where(mask[:, :, None, None], blocks[None], 0.0), axis=1)
+
+    owned = slice_owner[None, :] == index[:, None]
+    arranged = pick(owned, key_partial[0].reshape(groups, slice_rows, columns_key))
+    held_slice = jnp.sum(jnp.where(slice_owner == holder, index, 0))
+    old_slice = lax.dynamic_slice_in_dim(key_weight, held_slice * slice_rows, slice_rows, 0)
+    gradient, gathered, key_moment_new, key_second_new = chained(
+        expert_inputs[0],
+        hidden_grads[0],
+        arranged.astype(jnp.bfloat16),
+        old_slice,
+        key_moment[0],
+        key_second[0],
+    )
+    weight_next, moment_f, second_f = adam_update(
+        expert_weight[0], expert_moment[0], expert_second[0], gradient.astype(jnp.float32)
+    )
+    key_next = pick(owned.T, gathered).reshape(key_weight.shape)
+    return (
+        weight_next[None],
+        moment_f.astype(jnp.bfloat16)[None],
+        second_f.astype(jnp.bfloat16)[None],
+        key_next,
+        key_moment_new[None],
+        key_second_new[None],
+    )
+
+
 def solution(mesh):
     in_specs = (
         P("exp", "dp", None),
@@ -113,4 +526,5 @@
         P("exp", "dp", None),
         P("exp", "dp", None),
     )
-    return jax.shard_map(shards, mesh=mesh, in_specs=in_specs, out_specs=out_specs, check_vma=False)
+    body = line_shards if mesh.shape["dp"] == 2 * CHAIN else shards
+    return jax.shard_map(body, mesh=mesh, in_specs=in_specs, out_specs=out_specs, check_vma=False)

time: 338 us -> 222 us (0.66)
  waiting for transfers between devices: 270 us -> 0 us
  Pallas kernels: 0 us -> 198 us
  matrix products: 17.2 us -> 0 us
  between operations: 16.2 us -> 1.31 us
  blocking collectives: 9.99 us -> 0 us
    reduce_scatter x1 -> x0, waiting for transfers between devices: 240 us -> none  [shards(): lax.psum_scatter(lax.dot_general(inputs, upstream, (((0,), (0,)), ((), ()...]
    pallas_call x0 -> x1, Pallas kernels: none -> 198 us  [chained(): pl.pallas_call(functools.partial(kernel, chunk), out_shape=(jax.ShapeDtyp...]
    unnamed x3 -> x0, waiting for transfers between devices: 29.5 us -> none
    dot_general x3 -> x0, matrix products: 17.2 us -> none  [the longest x1 14.5 us: shards(): lax.dot_general(inputs, upstream, (((0,), (0,)), ((), ())), preferred_ele...]
    all_gather x1 -> x0, blocking collectives: 9.99 us -> none  [shards(): lax.all_gather(slice_new, 'exp', axis=0, tiled=True)]
    reduce_sum x1 -> x3, other arithmetic: 0.63 us -> 5.5 us  [the longest x2 4.15 us: pick(): return jnp.sum(jnp.where(mask[:, :, None, None], blocks[None], 0.0), axis=1)]
  transfers between devices with their start and end apart: 2 -> 0, of which waited for: 2 -> 0; matrix products, arithmetic and copies ran while one was open for 7% -> 0% of each run, Pallas kernels for 0% -> 0%
where the time goes in v1:
time: 222 us
  Pallas kernels  198 us (89%)
  other arithmetic  21 us (9%)
    pallas_call x1, Pallas kernels, chained(): pl.pallas_call(functools.partial(kernel, chunk), out_shape=(jax.ShapeDtyp...  198 us
    broadcast_in_dim x1, other arithmetic, line_shards(): second_f.astype(jnp.bfloat16)[None]  14.7 us

profile of v1, /device:TPU:0, one launch (start us, length us, event | category | flops | bytes accessed | tf_op | source)
XLA Modules:
  0.0 221.9 jit_solution(3442446209387150201)
XLA Ops:
  0.6 0.0 copy-start
  0.7 1.4 fusion.9
  2.7 0.8 iota_compare_fusion
  3.5 0.0 copy-done
  3.5 0.7 constant_dynamic-slice_fusion.kold_ref
  4.1 2.0 select_reduce_fusion.1.karr_ref
  6.2 197.6 %shard_map.145 = (bf16[256,7168]{1,0:T(8,128)(2,1)}, f32[4,64,512]{2,1,0:T(8,128)}, f32[64,512]{1,0:T(8,128)}, f32[64,512]{1,0:T(8,128)}) custom-call(bf16[256,2048]{1,0:T(8,128)(2,1)} %bitcast.46, bf16[256,7168]{1,0:T(8,128)(2,1)} %bitcast.45, bf16[4,64,512]{2,1,0:T(8,128)(2,1)} %select_reduce_fusion.1.karr_ref, ...), custom_call_target="tpu_custom_call" | custom-call | flops 13153337344 | bytes 58720256 | tf_op jit(solution)/shard_map/pallas_call | solution.py:429
  203.7 2.1 select_reduce_fusion
  205.8 0.0 copy-start.2
  205.8 0.0 copy-start.1
  205.8 14.7 %fusion.7 = (bf16[1,256,7168]{2,1,0:T(8,128)(2,1)}, f32[1,256,7168]{2,1,0:T(8,128)}, bf16[1,256,7168]{2,1,0:T(8,128)(2,1)}) fusion(bf16[256,7168]{1,0:T(8,128)(2,1)} %get-tuple-element.10, bf16[1,256,7168]{2,1,0:T(8,128)(2,1)} %param.14, bf16[1,256,7168]{2,1,0:T(8,128)(2,1)} %param.13, f32[1,256,7168]{2,1,0:T(8,128)} %param.12), kind=kLoop, calls=%fused_computation.11 | loop fusion | flops 36700160 | bytes 33030144 | tf_op jit(solution)/shard_map/broadcast_in_dim | solution.py:501
  220.6 0.0 copy-done.2
  220.6 0.7 copy.18
  221.2 0.0 copy-done.1
  221.2 0.7 copy.19
Async XLA Ops:
  0.6 2.8 %copy-start = (f32[256,512]{1,0:T(8,128)S(1)}, f32[256,512]{1,0:T(8,128)}, u32[]{:S(2)}) copy-start(f32[256,512]{1,0:T(8,128)} %param.16) | copy-start | bytes 1572868
  205.8 14.7 %copy-start.2 = (f32[64,512]{1,0:T(8,128)S(1)}, f32[64,512]{1,0:T(8,128)}, u32[]{:S(2)}) copy-start(f32[64,512]{1,0:T(8,128)} %get-tuple-element.12) | copy-start | bytes 393220
  205.8 15.4 %copy-start.1 = (f32[64,512]{1,0:T(8,128)S(1)}, f32[64,512]{1,0:T(8,128)}, u32[]{:S(2)}) copy-start(f32[64,512]{1,0:T(8,128)} %get-tuple-element.13) | copy-start | bytes 393220

commit v2 on v1

--- a/solution.py
+++ b/solution.py
@@ -22,10 +22,10 @@
     second_new = (
         second_decay * second.astype(jnp.float32) + (1.0 - second_decay) * gradient * gradient
     )
-    moment_hat = moment_new / (1.0 - first_decay**STEP)
-    second_hat = second_new / (1.0 - second_decay**STEP)
-    param_new = param - learn_rate * (
-        moment_hat / (jnp.sqrt(second_hat) + epsilon) + weight_decay * param
+    moment_scale = learn_rate / (1.0 - first_decay**STEP)
+    second_scale = 1.0 / (1.0 - second_decay**STEP)
+    param_new = (1.0 - learn_rate * weight_decay) * param - (moment_scale * moment_new) / (
+        jnp.sqrt(second_scale * second_new) + epsilon
     )
     return (param_new, moment_new, second_new)
 
@@ -102,14 +102,15 @@
 
 def kernel(
     chunk,
-    in_ref,
+    in_hbm,
     hid_ref,
-    karr_ref,
-    kold_ref,
-    kmom_ref,
-    ksec_ref,
+    kpart_hbm,
+    kweight_hbm,
+    mask_ref,
+    kmom_hbm,
+    ksec_hbm,
     g_ref,
-    kall_ref,
+    knext_out,
     kmom_out,
     ksec_out,
     lhs,
@@ -118,7 +119,15 @@
     got,
     fwd,
     own,
+    karr_ref,
+    kall_ref,
     kgot,
+    in_ref,
+    kpart_ref,
+    kweight_ref,
+    kmom_ref,
+    ksec_ref,
+    load_sem,
     local_sem,
     swap_send,
     swap_recv,
@@ -272,7 +281,31 @@
             (source, place),
         )
 
+    slice_rows = kmom_ref.shape[0]
+
+    def picked(ref, holder):
+        return sum(
+            mask_ref[holder * groups + s] * ref[s * slice_rows : (s + 1) * slice_rows, :]
+            for s in range(groups)
+        )
+
     barrier = pltpu.get_barrier_semaphore()
+
+    loads = [
+        pltpu.make_async_copy(src, dst, load_sem.at[i])
+        for i, (src, dst) in enumerate(
+            (
+                (in_hbm, in_ref),
+                (kpart_hbm, kpart_ref),
+                (kweight_hbm, kweight_ref),
+                (kmom_hbm, kmom_ref),
+                (ksec_hbm, ksec_ref),
+            )
+        )
+    ]
+    for load in loads:
+        load.start()
+    local_copy(0).start()
 
     def greet(dev):
         pl.semaphore_signal(barrier, inc=1, device_id=dev, device_id_type=MESH)
@@ -292,10 +325,8 @@
         greet(near_dev)
         pl.semaphore_wait(barrier, groups + 1)
 
-    @pl.loop(0, count)
-    def _(c):
-        local_copy(c).start()
-        swap_copy(c).start()
+    swap_copy(0).start()
+    loads[0].wait()
 
     @pl.loop(0, 2 * CHAIN)
     def _(q):
@@ -304,10 +335,19 @@
 
     @pl.when(jnp.logical_not(middle))
     def _():
-        for k in range(3):
-            edge_copy(k).start()
+        edge_copy(0).start()
 
     lhs_swap.start()
+
+    @pl.loop(1, count)
+    def _(c):
+        local_copy(c).start()
+        swap_copy(c).start()
+
+    for load in loads[1:]:
+        load.wait()
+    for h in range(groups):
+        karr_ref[h] = picked(kpart_ref, h).astype(karr_ref.dtype)
     for d in range(1, groups):
         key_copy(d).start()
 
@@ -317,7 +357,8 @@
         total = karr_ref[exp].astype(jnp.float32)
         for d in range(1, groups):
             total += kgot[d - 1].astype(jnp.float32)
-        new, moment, second = adam_update(kold_ref[...], kmom_ref[...], ksec_ref[...], total)
+        old = picked(kweight_ref, exp)
+        new, moment, second = adam_update(old, kmom_ref[...], ksec_ref[...], total)
         kmom_out[...] = moment
         ksec_out[...] = second
         kall_ref[exp] = new
@@ -337,6 +378,14 @@
             swap_copy(c).wait_recv()
             factor_copy(c).start()
 
+            @pl.when(c == 0)
+            def _():
+                edge_copy(1).start()
+
+            @pl.when(c == 2)
+            def _():
+                edge_copy(2).start()
+
         lhs_swap.wait_recv()
         key_step()
 
@@ -354,14 +403,15 @@
 
     @pl.when(middle)
     def _():
-        for k in range(3):
+        def take(k):
             edge_copy(k).wait_recv()
             pass_copy(k).start()
+            pass_copy(k).wait_recv()
+
         lhs_swap.wait_recv()
-        for k in range(3):
-            pass_copy(k).wait_recv()
-
-        @pl.loop(0, count + 1)
+        take(0)
+
+        @pl.loop(0, count + 2)
         def _(c):
             @pl.when(c < count)
             def _():
@@ -370,16 +420,22 @@
                 factor_copy(c).wait_recv()
                 prod[c, 0:block, :] = matmul(far, c, 4 * tokens).astype(prod.dtype)
                 far_copy(c).start()
+
+                @pl.when(c == 0)
+                def _():
+                    take(1)
+
                 prod[c, block:, :] = matmul(inner, c, 4 * tokens).astype(prod.dtype)
                 near_copy(c).start()
 
-            @pl.when(c == 1)
+            @pl.when(c == 2)
             def _():
+                take(2)
                 key_step()
 
-            @pl.when(c > 0)
+            @pl.when(c >= 2)
             def _():
-                p = c - 1
+                p = c - 2
                 far_copy(p).wait_recv()
                 fwd[p] = (
                     matmul(outer, p, 2 * tokens) + got[p, 0:block, :].astype(jnp.float32)
@@ -402,6 +458,11 @@
         key_copy(d).wait_send()
         all_copy(d).wait_send()
         all_arrival(d).wait_recv()
+
+    for s in range(groups):
+        knext_out[s * slice_rows : (s + 1) * slice_rows, :] = sum(
+            mask_ref[h * groups + s] * kall_ref[h] for h in range(groups)
+        )
 
     @pl.loop(0, count)
     def _(c):
@@ -414,28 +475,35 @@
         ).wait_recv()
 
 
-def chained(inputs, upstream, arranged, key_old, key_moment, key_second):
+def chained(inputs, upstream, key_partial, key_weight, owner, key_moment, key_second):
     tokens, width = inputs.shape
     columns = upstream.shape[1]
     half = columns // 2
-    chunk = 256 if half % 256 == 0 else 128
+    chunk = 256
     count = half // chunk
     block = width // CHAIN
-    groups = arranged.shape[0]
+    groups = owner.shape[0]
+    index = jnp.arange(groups, dtype=jnp.int32)
+    mask = (owner[None, :] == index[:, None]).astype(jnp.float32).reshape(groups * groups, 1, 1)
+    mask = jnp.broadcast_to(mask, (groups * groups, 1, key_weight.shape[1]))
     vmem = pl.BlockSpec(memory_space=pltpu.VMEM)
-    hbm = pl.BlockSpec(memory_space=pl.ANY)
-    key_shape = jax.ShapeDtypeStruct(key_old.shape, jnp.float32)
+    hbm = pl.BlockSpec(memory_space=pltpu.HBM)
+    key_shape = jax.ShapeDtypeStruct(key_moment.shape, jnp.float32)
     dma = pltpu.SemaphoreType.DMA
+
+    def hold(x):
+        return pltpu.with_memory_space_constraint(x, pltpu.HBM)
+
     return pl.pallas_call(
         functools.partial(kernel, chunk),
         out_shape=(
             jax.ShapeDtypeStruct((width // (2 * CHAIN), columns), jnp.bfloat16),
-            jax.ShapeDtypeStruct((groups,) + key_old.shape, jnp.float32),
+            jax.ShapeDtypeStruct(key_weight.shape, jnp.float32),
             key_shape,
             key_shape,
         ),
-        in_specs=[vmem, hbm, vmem, vmem, vmem, vmem],
-        out_specs=(hbm, vmem, vmem, vmem),
+        in_specs=[hbm, hbm, hbm, hbm, vmem, hbm, hbm],
+        out_specs=(pl.BlockSpec(memory_space=pl.ANY), vmem, vmem, vmem),
         scratch_shapes=[
             pltpu.VMEM((width, 4 * tokens), jnp.bfloat16),
             pltpu.VMEM((count, 4 * tokens, chunk), jnp.bfloat16),
@@ -443,19 +511,27 @@
             pltpu.VMEM((count, 2 * block, chunk), jnp.bfloat16),
             pltpu.VMEM((count, block, chunk), jnp.bfloat16),
             pltpu.VMEM((count, block, chunk), jnp.bfloat16),
-            pltpu.VMEM((groups - 1,) + key_old.shape, jnp.bfloat16),
+            pltpu.VMEM((groups,) + key_moment.shape, jnp.bfloat16),
+            pltpu.VMEM((groups,) + key_moment.shape, jnp.float32),
+            pltpu.VMEM((groups - 1,) + key_moment.shape, jnp.bfloat16),
+            pltpu.VMEM(inputs.shape, jnp.bfloat16),
+            pltpu.VMEM(key_partial.shape, jnp.float32),
+            pltpu.VMEM(key_weight.shape, jnp.float32),
+            pltpu.VMEM(key_moment.shape, jnp.float32),
+            pltpu.VMEM(key_second.shape, jnp.float32),
+            dma((5,)),
         ]
         + [dma((count,))] * 12
         + [dma, dma]
         + [dma((3,))] * 4
         + [dma((groups - 1,))] * 4,
         compiler_params=pltpu.CompilerParams(
-            collective_id=0, has_side_effects=True, vmem_limit_bytes=60 * 1024 * 1024
+            collective_id=0, has_side_effects=True, vmem_limit_bytes=38 * 1024 * 1024
         ),
         cost_estimate=pl.CostEstimate(
             flops=14 * block * block * half, bytes_accessed=4 * width * columns, transcendentals=0
         ),
-    )(inputs, upstream, arranged, key_old, key_moment, key_second)
+    )(*(hold(x) for x in (inputs, upstream, key_partial, key_weight)), mask, hold(key_moment), hold(key_second))
 
 
 def line_shards(
@@ -470,31 +546,18 @@
     key_second,
     slice_owner,
 ):
-    groups = lax.axis_size("exp")
-    holder = lax.axis_index("exp")
-    slice_rows = key_weight.shape[0] // groups
-    columns_key = key_weight.shape[1]
-    index = jnp.arange(groups, dtype=jnp.int32)
-
-    def pick(mask, blocks):
-        return jnp.sum(jnp.where(mask[:, :, None, None], blocks[None], 0.0), axis=1)
-
-    owned = slice_owner[None, :] == index[:, None]
-    arranged = pick(owned, key_partial[0].reshape(groups, slice_rows, columns_key))
-    held_slice = jnp.sum(jnp.where(slice_owner == holder, index, 0))
-    old_slice = lax.dynamic_slice_in_dim(key_weight, held_slice * slice_rows, slice_rows, 0)
-    gradient, gathered, key_moment_new, key_second_new = chained(
+    gradient, key_next, key_moment_new, key_second_new = chained(
         expert_inputs[0],
         hidden_grads[0],
-        arranged.astype(jnp.bfloat16),
-        old_slice,
+        key_partial[0],
+        key_weight,
+        slice_owner,
         key_moment[0],
         key_second[0],
     )
     weight_next, moment_f, second_f = adam_update(
         expert_weight[0], expert_moment[0], expert_second[0], gradient.astype(jnp.float32)
     )
-    key_next = pick(owned.T, gathered).reshape(key_weight.shape)
     return (
         weight_next[None],
         moment_f.astype(jnp.bfloat16)[None],

time: 222 us -> 200 us (0.901)
  Pallas kernels: 198 us -> 186 us
  other arithmetic: 21 us -> 11.1 us
    pallas_call x1, Pallas kernels: 198 us -> 186 us  [chained(): pl.pallas_call(functools.partial(kernel, chunk), out_shape=(jax.ShapeDtyp...]
    reduce_sum x3 -> x0, other arithmetic: 5.5 us -> none  [the longest x2 4.15 us: pick(): return jnp.sum(jnp.where(mask[:, :, None, None], blocks[None], 0.0), axis=1)]
    broadcast_in_dim x1, other arithmetic: 14.7 us -> 10.5 us  [line_shards(): second_f.astype(jnp.bfloat16)[None]]
where the time goes in v2:
time: 200 us
  Pallas kernels  186 us (93%)
  other arithmetic  11.1 us (6%)
  local copies, waits for them, and re-layouts  2.29 us (1%)
    pallas_call x1, Pallas kernels, chained(): pl.pallas_call(functools.partial(kernel, chunk), out_shape=(jax.ShapeDtyp...  186 us
    broadcast_in_dim x1, other arithmetic, line_shards(): second_f.astype(jnp.bfloat16)[None]  10.5 us

profile of v2, /device:TPU:0, one launch (start us, length us, event | category | flops | bytes accessed | tf_op | source)
XLA Modules:
  0.0 200.3 jit_solution(11296469564362810040)
XLA Ops:
  0.6 0.7 fusion.7
  1.3 0.1 reshape.41
  1.4 0.1 broadcast_in_dim.22.mask_ref
  1.5 0.0 copy-start
  1.5 0.0 copy-start.1
  1.5 0.0 copy-start.2
  1.5 186.2 %shard_map.145 = (bf16[256,7168]{1,0:T(8,128)(2,1)S(1)}, f32[256,512]{1,0:T(8,128)S(1)}, f32[64,512]{1,0:T(8,128)S(1)}, f32[64,512]{1,0:T(8,128)S(1)}) custom-call(bf16[256,2048]{1,0:T(8,128)(2,1)} %bitcast.36, bf16[256,7168]{1,0:T(8,128)(2,1)} %bitcast.35, f32[256,512]{1,0:T(8,128)} %bitcast.37, f32[256,512]{1,0:T(8,128)} %kweight_hbm.1, ...), custom_call_target="tpu_custom_call" | custom-call | flops 13153337344 | bytes 58720256 | tf_op jit(solution)/shard_map/pallas_call | solution.py:497
  187.7 0.0 copy-done
  187.7 0.0 copy-done.1
  187.7 0.0 copy-done.2
  187.8 10.5 %fusion.5 = (bf16[1,256,7168]{2,1,0:T(8,128)(2,1)}, f32[1,256,7168]{2,1,0:T(8,128)}, bf16[1,256,7168]{2,1,0:T(8,128)(2,1)}) fusion(bf16[256,7168]{1,0:T(8,128)(2,1)S(1)} %get-tuple-element.10, bf16[1,256,7168]{2,1,0:T(8,128)(2,1)S(1)} %copy-done.1, bf16[1,256,7168]{2,1,0:T(8,128)(2,1)S(1)} %copy-done.2, f32[1,256,7168]{2,1,0:T(8,128)S(1)} %copy-done), kind=kLoop, calls=%fused_computation.8 | loop fusion | flops 33030144 | bytes 33030144 | tf_op jit(solution)/shard_map/broadcast_in_dim | solution.py:564
  198.2 0.8 copy.19
  199.0 0.7 copy.20
  199.7 0.7 copy.21
Async XLA Ops:
  1.5 186.3 %copy-start = (f32[1,256,7168]{2,1,0:T(8,128)S(1)}, f32[1,256,7168]{2,1,0:T(8,128)}, u32[]{:S(2)}) copy-start(f32[1,256,7168]{2,1,0:T(8,128)} %param.12) | copy-start | bytes 22020100
  1.5 186.3 %copy-start.1 = (bf16[1,256,7168]{2,1,0:T(8,128)(2,1)S(1)}, bf16[1,256,7168]{2,1,0:T(8,128)(2,1)}, u32[]{:S(2)}) copy-start(bf16[1,256,7168]{2,1,0:T(8,128)(2,1)} %param.14) | copy-start | bytes 11010052
  1.5 186.2 %copy-start.2 = (bf16[1,256,7168]{2,1,0:T(8,128)(2,1)S(1)}, bf16[1,256,7168]{2,1,0:T(8,128)(2,1)}, u32[]{:S(2)}) copy-start(bf16[1,256,7168]{2,1,0:T(8,128)(2,1)} %param.13) | copy-start | bytes 11010052
